TPU v7x, 256 devices: a whole 4x4x8 slice. The times are simulated.
256 devices in a mesh: dp: 32 (over z, x), proto: 8 (over y, core).
Axes of the slice: x: 4, y: 4, z: 8, core: 2. Of those that a mesh axis runs over, the one named last changes fastest.
Arguments:
- centroids: bfloat16 [131072, 768], P(('dp', 'proto')), may hold values from -1 to 1
- queries: bfloat16 [4096, 768], P('dp'), may hold values from -40 to 40
- positive: int32 [4096], P('dp'), may hold values from 0 to 131071
- members: bfloat16 [32, 32, 8, 16, 768], P('dp'), may hold values from -0.29882812 to 0.29882812
- member_slot: int32 [32, 32, 8, 16], P('dp'), may hold values from 0 to 511
- block_count: int32 [32, 32, 8], P('dp'), may hold values from 0 to 16, as said below
Outputs:
- concentration: float32 [131072], P(('dp', 'proto'))
- loss: float32 [4096], P('dp')
- query_grad: bfloat16 [4096, 768], P('dp')
Inputs may be any that keep to these rules, and one draw needn't show every extreme that they name: `block_count`: some block is full from every source group; the used slots come first in each block.
All inputs are finite; a program needn't handle non-finite values.
Results may differ from a plain program's by a relative error of at most 0.0056.
Values may be sent and summed in bfloat16 or wider, within the bound.
A program may use at most 128 MiB of HBM per device.

v0:
```python
import jax
import jax.numpy as jnp
from jax import lax
from jax.sharding import PartitionSpec as P


def on_device(centroids, queries, positive, members, member_slot, block_count):
    width = centroids.shape[1]
    cent_local = centroids.shape[0]
    q_local = queries.shape[0]
    column = lax.axis_index("proto")
    flat_index = lax.axis_index("dp") * lax.axis_size("proto") + column
    member_mine = lax.dynamic_index_in_dim(members, column, 2, keepdims=False)
    slot_mine = lax.dynamic_index_in_dim(member_slot, column, 2, keepdims=False)
    count_mine = lax.dynamic_index_in_dim(block_count, column, 2, keepdims=False)
    arrived, arrived_slot, arrived_count = (
        lax.all_to_all(member_mine, "dp", split_axis=1, concat_axis=0, tiled=True),
        lax.all_to_all(slot_mine, "dp", split_axis=1, concat_axis=0, tiled=True),
        lax.all_to_all(count_mine, "dp", split_axis=1, concat_axis=0, tiled=True),
    )
    slots_per = arrived.shape[2]
    member_rows = arrived.reshape(-1, width)
    slot_flat = arrived_slot.reshape(-1)
    valid = (
        (jnp.arange(slots_per, dtype=jnp.int32)[None, None, :] < arrived_count[:, :, None])
        .astype(jnp.float32)
        .reshape(-1)
    )
    picked = jnp.take(centroids, slot_flat, axis=0).astype(jnp.float32)
    distance = jnp.sqrt(jnp.sum((member_rows.astype(jnp.float32) - picked) ** 2, axis=1) + 1e-06)
    onehot = (jnp.arange(cent_local, dtype=jnp.int32)[:, None] == slot_flat[None, :]).astype(
        jnp.float32
    )
    total = jnp.dot(onehot, distance * valid, precision=lax.Precision.HIGHEST)
    counted = jnp.dot(onehot, valid, precision=lax.Precision.HIGHEST)
    concentration = (total + 1.0) / ((counted + 1.0) * jnp.log(counted + 10.0))
    inverse = 1.0 / concentration
    all_queries, all_positive = (
        lax.all_gather(queries, "dp", axis=0, tiled=True),
        lax.all_gather(positive, "dp", axis=0, tiled=True),
    )
    scores = (
        lax.dot_general(
            all_queries, centroids, (((1,), (1,)), ((), ())), preferred_element_type=jnp.float32
        )
        * inverse[None, :]
    )
    local_positive = all_positive - flat_index * cent_local
    positive_hit = (
        jnp.arange(cent_local, dtype=jnp.int32)[None, :] == local_positive[:, None]
    ).astype(jnp.float32)
    target_part = jnp.sum(scores * positive_hit, axis=1)
    local_max = jnp.max(scores, axis=1)
    row_max = lax.pmax(local_max, ("dp", "proto"))
    local_sum = jnp.sum(jnp.exp(scores - row_max[:, None]), axis=1)
    row_sum, target = lax.psum((local_sum, target_part), ("dp", "proto"))
    loss_all = row_max + jnp.log(row_sum) - target
    loss_mine = lax.dynamic_slice_in_dim(loss_all, lax.axis_index("dp") * q_local, q_local)
    probs = jnp.exp(scores - row_max[:, None]) / row_sum[:, None]
    weight = ((probs - positive_hit) * inverse[None, :]).astype(jnp.bfloat16)
    partial_rows = lax.psum_scatter(
        jnp.dot(weight, centroids, preferred_element_type=jnp.float32),
        "dp",
        scatter_dimension=0,
        tiled=True,
    )
    summed = lax.psum(partial_rows, "proto")
    return (concentration, loss_mine, summed.astype(jnp.bfloat16))


def solution(mesh):
    placed = (
        P(("dp", "proto"), None),
        P("dp", None),
        P("dp"),
        P("dp", None, None, None, None),
        P("dp", None, None, None),
        P("dp", None, None),
    )
    return jax.shard_map(
        on_device,
        mesh=mesh,
        in_specs=placed,
        out_specs=(P(("dp", "proto")), P("dp"), P("dp", None)),
        check_vma=False,
    )
```

profile of v0, /device:TPU:2, one launch (start us, length us, event | category | flops | bytes accessed | tf_op | source)
XLA Modules:
  0.0 548.8 jit_solution(13499479848178516080)
XLA Ops:
  7.2 0.0 copy-start
  7.2 0.0 all-gather.3.cloned.1.call-start
  7.2 0.7 all-gather.3.cloned.1.call-update
  7.9 0.7 constant_dynamic-slice_fusion
  8.6 0.7 copy.28
  9.3 11.6 %all-to-all-start.1 = ((s32[1,32,1]{2,0,1:T(1,128)}), s32[1,32,1]{2,0,1:T(1,128)S(1)}, u32[]{:S(2)}, u32[]{:S(2)}) async-start(s32[1,32,1]{2,0,1:T(1,128)} %copy.28), calls=%async_computation.1 | async-start | bytes 32768 | tf_op jit(solution)/shard_map/all_to_all | solution.py:19
  20.9 0.7 constant_dynamic-slice_fusion.1
  21.6 0.7 copy.23
  22.3 7.1 %all-to-all-done.1 = s32[1,32,1]{2,0,1:T(1,128)S(1)} async-done(((s32[1,32,1]{2,0,1:T(1,128)}), s32[1,32,1]{2,0,1:T(1,128)S(1)}, u32[]{:S(2)}, u32[]{:S(2)}) %all-to-all-start.1) | async-done | bytes 160 | tf_op jit(solution)/shard_map/all_to_all | solution.py:19
  29.4 4.9 all-to-all-start
  34.3 2.1 dynamic-slice_bitcast_fusion
  36.4 6.6 %all-to-all-done = s32[1,32,16]{2,0,1:T(1,128)S(1)} async-done(((s32[1,32,16]{2,0,1:T(1,128)}), s32[1,32,16]{2,0,1:T(1,128)S(1)}, u32[]{:S(2)}, u32[]{:S(2)}) %all-to-all-start) | async-done | bytes 2080 | tf_op jit(solution)/shard_map/all_to_all | solution.py:18
  43.0 4.9 all-to-all-start.2
  48.0 0.0 reduce-scatter.2.cloned.1.call-start
  48.0 49.9 %all-gather = s32[32,1,128]{2,1,0:T(1,128)S(1)} all-gather(s32[1,1,128]{2,1,0:T(1,128)} %bitcast.42), channel_id=1, replica_groups=mesh['dp'=32,'proto'=8] {'dp'}, dimensions={0}, use_global_device_ids=true | all-gather | bytes 16896 | tf_op jit(solution)/shard_map/all_gather | solution.py:40
  97.9 0.7 reduce.4
  98.6 0.1 iota_compare_fusion.4
  98.6 0.1 lt.61
  98.7 0.1 reshape.139
  98.8 0.1 reshape.124
  98.9 0.5 broadcast.91
  99.4 0.7 reduce.9
  100.1 0.1 eq.31
  100.2 0.1 copy.25
  100.3 0.1 copy.26
  100.4 0.0 copy-done
  100.4 2.0 gather_fusion
  102.4 0.3 fusion.2
  102.7 0.0 all-to-all-done.2
  102.7 0.5 multiply_reduce_fusion.1
  103.3 0.1 sqrt.7
  103.4 0.6 fusion.3
  103.9 0.6 add_divide_fusion
  104.5 0.0 all-gather.3.cloned.1.call-done
  104.5 8.4 %multiply_reduce_fusion = (f32[4096]{0:T(1024)S(1)}, f32[4096,512]{0,1:T(8,128)}) fusion(f32[512]{0:T(512)S(1)} %get-tuple-element.7, bf16[4096,768]{1,0:T(8,128)(2,1)} %all-gather.3.cloned.1.call-done, bf16[512,768]{1,0:T(8,128)(2,1)S(1)} %copy-done), kind=kOutput, calls=%fused_computation.6 | convolution fusion | flops 3225415680 | bytes 15484928 | tf_op jit(solution)/shard_map/dot_general | solution.py:43
  112.9 73.2 %pmax.7 = f32[4096]{0:T(1024)S(1)} all-reduce(f32[4096]{0:T(1024)S(1)} %get-tuple-element.9), channel_id=1, replica_groups=mesh['dp'=32,'proto'=8] {'dp','proto'}, use_global_device_ids=true, to_apply=%region_2.3 | all-reduce | flops 4096 | bytes 32768 | tf_op jit(solution)/shard_map/pmax | solution.py:54
  186.1 5.0 fusion
  191.1 74.7 %all-reduce = (f32[4096]{0:T(1024)S(1)}, f32[4096]{0:T(1024)S(1)}) all-reduce(f32[4096]{0:T(1024)S(1)} %get-tuple-element.4, f32[4096]{0:T(1024)S(1)} %get-tuple-element.3), channel_id=1, replica_groups=mesh['dp'=32,'proto'=8] {'dp','proto'}, use_global_device_ids=true, to_apply=%region_6.7 | all-reduce | flops 8192 | bytes 65536 | tf_op jit(solution)/shard_map/psum | solution.py:56
  265.8 13.1 %fusion.1 = f32[4096,768]{1,0:T(8,128)} fusion(bf16[512,768]{1,0:T(8,128)(2,1)S(1)} %copy-done, f32[4096,512]{0,1:T(8,128)} %get-tuple-element.10, f32[4096]{0:T(1024)S(1)} %get-tuple-element.6, s32[4096]{0:T(1024)S(1)} %bitcast.36, f32[4096]{0:T(1024)S(1)} %pmax.7, f32[512]{0:T(512)S(1)} %get-tuple-element.7), kind=kOutput, calls=%fused_computation.7 | convolution fusion | flops 3238002688 | bytes 21809152 | tf_op jit(solution)/shard_map/dot_general | solution.py:62
  278.9 0.0 reduce-scatter.2.cloned.1.call-update
  278.9 0.6 dynamic-slice_subtract_fusion
  279.5 233.8 %reduce-scatter.2.cloned.1.call-done = f32[128,768]{1,0:T(8,128)} async-done(((f32[4096,768]{1,0:T(8,128)}), f32[128,768]{1,0:T(8,128)}) %reduce-scatter.2.cloned.1.call-update) | async-done | bytes 393232 | tf_op jit(solution)/shard_map/reduce_scatter | solution.py:61
  513.2 28.7 %all-reduce.2 = bf16[128,768]{1,0:T(8,128)(2,1)} all-reduce(f32[128,768]{1,0:T(8,128)} %reduce-scatter.2.cloned.1.call-done), channel_id=1, replica_groups=mesh['dp'=32,'proto'=8] {'proto'}, use_global_device_ids=true, to_apply=%region_8.9 | all-reduce | flops 98304 | bytes 589824 | tf_op jit(solution)/shard_map/psum | solution.py:67
  (6 shorter events, 0.0 us)
Async XLA Ops:
  7.2 93.2 %copy-start = (bf16[512,768]{1,0:T(8,128)(2,1)S(1)}, bf16[512,768]{1,0:T(8,128)(2,1)}, u32[]{:S(2)}) copy-start(bf16[512,768]{1,0:T(8,128)(2,1)} %param.6) | copy-start | bytes 2359300
  7.2 97.3 %all-gather.3.cloned.1.call-start = ((), (), s32[]{:S(2)}) async-start(), calls=%async_computation.4 | async-start | bytes 6488064 | tf_op jit(solution)/shard_map/all_gather | solution.py:39
  9.3 20.1 %all-to-all-start.1 = ((s32[1,32,1]{2,0,1:T(1,128)}), s32[1,32,1]{2,0,1:T(1,128)S(1)}, u32[]{:S(2)}, u32[]{:S(2)}) async-start(s32[1,32,1]{2,0,1:T(1,128)} %copy.28), calls=%async_computation.1 | async-start | bytes 32768 | tf_op jit(solution)/shard_map/all_to_all | solution.py:19
  29.4 13.6 %all-to-all-start = ((s32[1,32,16]{2,0,1:T(1,128)}), s32[1,32,16]{2,0,1:T(1,128)S(1)}, u32[]{:S(2)}, u32[]{:S(2)}) async-start(s32[1,32,16]{2,0,1:T(1,128)} %bitcast), calls=%async_computation | async-start | bytes 32768 | tf_op jit(solution)/shard_map/all_to_all | solution.py:18
  43.0 59.7 %all-to-all-start.2 = ((bf16[1,32,16,768]{3,2,0,1:T(8,128)(2,1)}), bf16[1,32,16,768]{3,2,0,1:T(8,128)(2,1)S(1)}, u32[]{:S(2)}, u32[]{:S(2)}) async-start(bf16[1,32,16,768]{3,2,0,1:T(8,128)(2,1)} %dynamic-slice_bitcast_fusion), calls=%async_computation.2 | async-start | bytes 1572864 | tf_op jit(solution)/shard_map/all_to_all | solution.py:17
  48.0 465.3 %reduce-scatter.2.cloned.1.call-start = ((), (), s32[]{:S(2)}) async-start(), calls=%async_computation.5 | async-start | bytes 12976128 | tf_op jit(solution)/shard_map/reduce_scatter | solution.py:61
Sparse Core Ops, SparseCore 0:
  10.6 91.8 all-gather.2
  279.0 234.1 reduce-scatter.1
where the time goes:
time: 550 us; the launch traced here: 549 us
  waiting for transfers between devices  248 us (45%)
  blocking collectives  226 us (41%)
  matrix products  22.3 us (4%)
  starting transfers between devices  21.5 us (4%)
  between operations  14.2 us (3%)
  other arithmetic  8.13 us (1%)
  local copies, waits for them, and re-layouts  7.99 us (1%)
    reduce_scatter x1, waiting for transfers between devices, on_device(): lax.psum_scatter(jnp.dot(weight, centroids, preferred_element_type=jnp.fl...  234 us
    psum x1, blocking collectives, on_device(): row_sum, target = lax.psum((local_sum, target_part), ('dp', 'proto'))  74.7 us
    pmax x1, blocking collectives, on_device(): row_max = lax.pmax(local_max, ('dp', 'proto'))  73.2 us
    all_gather x1, blocking collectives, on_device(): lax.all_gather(positive, 'dp', axis=0, tiled=True)  49.9 us
    psum x1, blocking collectives, on_device(): summed = lax.psum(partial_rows, 'proto')  28.7 us
    dot_general x1, matrix products, on_device(): jnp.dot(weight, centroids, preferred_element_type=jnp.float32)  13.1 us
    all_to_all x1, starting transfers between devices, on_device(): lax.all_to_all(count_mine, 'dp', split_axis=1, concat_axis=0, tiled=True)  11.6 us
  transfers between devices with their start and end apart: 5, of which 3 were waited for; matrix products, arithmetic and copies ran while one was open for 2% of the time, Pallas kernels for 0%

commit v1 on v0

--- a/solution.py
+++ b/solution.py
@@ -2,6 +2,11 @@
 import jax.numpy as jnp
 from jax import lax
 from jax.sharding import PartitionSpec as P
+
+
+def one_after_other(value, axis_one, axis_two):
+    half = lax.psum(value, axis_one)
+    return lax.psum(half, axis_two)
 
 
 def on_device(centroids, queries, positive, members, member_slot, block_count):
@@ -53,7 +58,7 @@
     local_max = jnp.max(scores, axis=1)
     row_max = lax.pmax(local_max, ("dp", "proto"))
     local_sum = jnp.sum(jnp.exp(scores - row_max[:, None]), axis=1)
-    row_sum, target = lax.psum((local_sum, target_part), ("dp", "proto"))
+    row_sum, target = one_after_other((local_sum, target_part), "proto", "dp")
     loss_all = row_max + jnp.log(row_sum) - target
     loss_mine = lax.dynamic_slice_in_dim(loss_all, lax.axis_index("dp") * q_local, q_local)
     probs = jnp.exp(scores - row_max[:, None]) / row_sum[:, None]

time: 550 us -> 638 us (1.16)
  blocking collectives: 226 us -> 312 us
    psum x1 -> x2, blocking collectives: 74.7 us -> 161 us  [the longest x1 136 us: one_after_other(): return lax.psum(half, axis_two)]
where the time goes in v1:
time: 638 us; the launch traced here: 637 us
  blocking collectives  312 us (49%)
  waiting for transfers between devices  251 us (39%)
  matrix products  22.3 us (3%)
  starting transfers between devices  21.5 us (3%)
  between operations  14.2 us (2%)
  other arithmetic  8.13 us (1%)
  local copies, waits for them, and re-layouts  7.99 us (1%)
    reduce_scatter x1, waiting for transfers between devices, on_device(): lax.psum_scatter(jnp.dot(weight, centroids, preferred_element_type=jnp.fl...  236 us
    psum x1, blocking collectives, one_after_other(): return lax.psum(half, axis_two)  136 us
    pmax x1, blocking collectives, on_device(): row_max = lax.pmax(local_max, ('dp', 'proto'))  73.2 us
    all_gather x1, blocking collectives, on_device(): lax.all_gather(positive, 'dp', axis=0, tiled=True)  49.9 us
    psum x1, blocking collectives, on_device(): summed = lax.psum(partial_rows, 'proto')  28.7 us
    psum x1, blocking collectives, one_after_other(): half = lax.psum(value, axis_one)  24.8 us
    dot_general x1, matrix products, on_device(): jnp.dot(weight, centroids, preferred_element_type=jnp.float32)  13.1 us
  transfers between devices with their start and end apart: 5, of which 3 were waited for; matrix products, arithmetic and copies ran while one was open for 2% of the time, Pallas kernels for 0%

profile of v1, /device:TPU:2, one launch (start us, length us, event | category | flops | bytes accessed | tf_op | source)
XLA Modules:
  0.0 637.2 jit_solution(352925320475696971)
XLA Ops:
  7.2 0.0 copy-start
  7.2 0.0 all-gather.3.cloned.1.call-start
  7.2 0.7 all-gather.3.cloned.1.call-update
  7.9 0.7 constant_dynamic-slice_fusion
  8.6 0.7 copy.28
  9.3 11.6 %all-to-all-start.1 = ((s32[1,32,1]{2,0,1:T(1,128)}), s32[1,32,1]{2,0,1:T(1,128)S(1)}, u32[]{:S(2)}, u32[]{:S(2)}) async-start(s32[1,32,1]{2,0,1:T(1,128)} %copy.28), calls=%async_computation.1 | async-start | bytes 32768 | tf_op jit(solution)/shard_map/all_to_all | solution.py:24
  20.9 0.7 constant_dynamic-slice_fusion.1
  21.6 0.7 copy.23
  22.3 7.1 %all-to-all-done.1 = s32[1,32,1]{2,0,1:T(1,128)S(1)} async-done(((s32[1,32,1]{2,0,1:T(1,128)}), s32[1,32,1]{2,0,1:T(1,128)S(1)}, u32[]{:S(2)}, u32[]{:S(2)}) %all-to-all-start.1) | async-done | bytes 160 | tf_op jit(solution)/shard_map/all_to_all | solution.py:24
  29.4 4.9 all-to-all-start
  34.3 2.1 dynamic-slice_bitcast_fusion
  36.4 6.6 %all-to-all-done = s32[1,32,16]{2,0,1:T(1,128)S(1)} async-done(((s32[1,32,16]{2,0,1:T(1,128)}), s32[1,32,16]{2,0,1:T(1,128)S(1)}, u32[]{:S(2)}, u32[]{:S(2)}) %all-to-all-start) | async-done | bytes 2080 | tf_op jit(solution)/shard_map/all_to_all | solution.py:23
  43.0 4.9 all-to-all-start.2
  48.0 0.0 reduce-scatter.2.cloned.1.call-start
  48.0 49.9 %all-gather = s32[32,1,128]{2,1,0:T(1,128)S(1)} all-gather(s32[1,1,128]{2,1,0:T(1,128)} %bitcast.42), channel_id=1, replica_groups=mesh['dp'=32,'proto'=8] {'dp'}, dimensions={0}, use_global_device_ids=true | all-gather | bytes 16896 | tf_op jit(solution)/shard_map/all_gather | solution.py:45
  97.9 0.7 reduce.4
  98.6 0.1 iota_compare_fusion.4
  98.6 0.1 lt.61
  98.7 0.1 reshape.139
  98.8 0.1 reshape.124
  98.9 0.5 broadcast.91
  99.4 0.7 reduce.9
  100.1 0.1 eq.31
  100.2 0.1 copy.25
  100.3 0.1 copy.26
  100.4 0.0 copy-done
  100.4 2.0 gather_fusion
  102.4 0.3 fusion.2
  102.7 0.0 all-to-all-done.2
  102.7 0.5 multiply_reduce_fusion.1
  103.3 0.1 sqrt.7
  103.4 0.6 fusion.3
  103.9 0.6 add_divide_fusion
  104.5 0.0 all-gather.3.cloned.1.call-done
  104.5 8.4 %multiply_reduce_fusion = (f32[4096]{0:T(1024)S(1)}, f32[4096,512]{0,1:T(8,128)}) fusion(f32[512]{0:T(512)S(1)} %get-tuple-element.9, bf16[4096,768]{1,0:T(8,128)(2,1)} %all-gather.3.cloned.1.call-done, bf16[512,768]{1,0:T(8,128)(2,1)S(1)} %copy-done), kind=kOutput, calls=%fused_computation.6 | convolution fusion | flops 3225415680 | bytes 15484928 | tf_op jit(solution)/shard_map/dot_general | solution.py:48
  112.9 73.2 %pmax.7 = f32[4096]{0:T(1024)S(1)} all-reduce(f32[4096]{0:T(1024)S(1)} %get-tuple-element.11), channel_id=1, replica_groups=mesh['dp'=32,'proto'=8] {'dp','proto'}, use_global_device_ids=true, to_apply=%region_2.3 | all-reduce | flops 4096 | bytes 32768 | tf_op jit(solution)/shard_map/pmax | solution.py:59
  186.1 5.0 fusion
  191.1 24.8 %all-reduce.1 = (f32[4096]{0:T(1024)S(1)}, f32[4096]{0:T(1024)S(1)}) all-reduce(f32[4096]{0:T(1024)S(1)} %get-tuple-element.4, f32[4096]{0:T(1024)S(1)} %get-tuple-element.3), channel_id=1, replica_groups=mesh['dp'=32,'proto'=8] {'proto'}, use_global_device_ids=true, to_apply=%region_7.8 | all-reduce | flops 8192 | bytes 65536 | tf_op jit(solution)/shard_map/psum | solution.py:8
  215.9 135.8 %all-reduce = (f32[4096]{0:T(1024)S(1)}, f32[4096]{0:T(1024)S(1)}) all-reduce(f32[4096]{0:T(1024)S(1)} %get-tuple-element.7, f32[4096]{0:T(1024)S(1)} %get-tuple-element.8), channel_id=1, replica_groups=mesh['dp'=32,'proto'=8] {'dp'}, use_global_device_ids=true, to_apply=%region_8.9 | all-reduce | flops 8192 | bytes 65536 | tf_op jit(solution)/shard_map/psum | solution.py:9
  351.7 13.1 %fusion.1 = f32[4096,768]{1,0:T(8,128)} fusion(bf16[512,768]{1,0:T(8,128)(2,1)S(1)} %copy-done, f32[4096,512]{0,1:T(8,128)} %get-tuple-element.12, f32[4096]{0:T(1024)S(1)} %get-tuple-element.6, s32[4096]{0:T(1024)S(1)} %bitcast.36, f32[4096]{0:T(1024)S(1)} %pmax.7, f32[512]{0:T(512)S(1)} %get-tuple-element.9), kind=kOutput, calls=%fused_computation.7 | convolution fusion | flops 3238002688 | bytes 21809152 | tf_op jit(solution)/shard_map/dot_general | solution.py:67
  364.8 0.0 reduce-scatter.2.cloned.1.call-update
  364.8 0.6 dynamic-slice_subtract_fusion
  365.4 236.2 %reduce-scatter.2.cloned.1.call-done = f32[128,768]{1,0:T(8,128)} async-done(((f32[4096,768]{1,0:T(8,128)}), f32[128,768]{1,0:T(8,128)}) %reduce-scatter.2.cloned.1.call-update) | async-done | bytes 393232 | tf_op jit(solution)/shard_map/reduce_scatter | solution.py:66
  601.6 28.7 %all-reduce.3 = bf16[128,768]{1,0:T(8,128)(2,1)} all-reduce(f32[128,768]{1,0:T(8,128)} %reduce-scatter.2.cloned.1.call-done), channel_id=1, replica_groups=mesh['dp'=32,'proto'=8] {'proto'}, use_global_device_ids=true, to_apply=%region_10.11 | all-reduce | flops 98304 | bytes 589824 | tf_op jit(solution)/shard_map/psum | solution.py:72
  (6 shorter events, 0.0 us)
Async XLA Ops:
  7.2 93.2 %copy-start = (bf16[512,768]{1,0:T(8,128)(2,1)S(1)}, bf16[512,768]{1,0:T(8,128)(2,1)}, u32[]{:S(2)}) copy-start(bf16[512,768]{1,0:T(8,128)(2,1)} %param.6) | copy-start | bytes 2359300
  7.2 97.3 %all-gather.3.cloned.1.call-start = ((), (), s32[]{:S(2)}) async-start(), calls=%async_computation.4 | async-start | bytes 6488064 | tf_op jit(solution)/shard_map/all_gather | solution.py:44
  9.3 20.1 %all-to-all-start.1 = ((s32[1,32,1]{2,0,1:T(1,128)}), s32[1,32,1]{2,0,1:T(1,128)S(1)}, u32[]{:S(2)}, u32[]{:S(2)}) async-start(s32[1,32,1]{2,0,1:T(1,128)} %copy.28), calls=%async_computation.1 | async-start | bytes 32768 | tf_op jit(solution)/shard_map/all_to_all | solution.py:24
  29.4 13.6 %all-to-all-start = ((s32[1,32,16]{2,0,1:T(1,128)}), s32[1,32,16]{2,0,1:T(1,128)S(1)}, u32[]{:S(2)}, u32[]{:S(2)}) async-start(s32[1,32,16]{2,0,1:T(1,128)} %bitcast), calls=%async_computation | async-start | bytes 32768 | tf_op jit(solution)/shard_map/all_to_all | solution.py:23
  43.0 59.7 %all-to-all-start.2 = ((bf16[1,32,16,768]{3,2,0,1:T(8,128)(2,1)}), bf16[1,32,16,768]{3,2,0,1:T(8,128)(2,1)S(1)}, u32[]{:S(2)}, u32[]{:S(2)}) async-start(bf16[1,32,16,768]{3,2,0,1:T(8,128)(2,1)} %dynamic-slice_bitcast_fusion), calls=%async_computation.2 | async-start | bytes 1572864 | tf_op jit(solution)/shard_map/all_to_all | solution.py:22
  48.0 553.7 %reduce-scatter.2.cloned.1.call-start = ((), (), s32[]{:S(2)}) async-start(), calls=%async_computation.5 | async-start | bytes 12976128 | tf_op jit(solution)/shard_map/reduce_scatter | solution.py:66
Sparse Core Ops, SparseCore 0:
  10.6 91.8 all-gather.2
  365.0 236.6 reduce-scatter.1
